TPU v7x, 256 devices: a whole 4x4x8 slice. The times are simulated.
256 devices in a mesh: seq: 32 (over z, x), mp: 8 (over y, core).
Axes of the slice: x: 4, y: 4, z: 8, core: 2. Of those that a mesh axis runs over, the one named last changes fastest.
Arguments:
- win_query: bfloat16 [16384, 4096], P('seq', 'mp'), may hold values from -8 to 8
- win_key: bfloat16 [16384, 4096], P('seq', 'mp'), may hold values from -8 to 8
- win_value: bfloat16 [16384, 4096], P('seq', 'mp'), may hold values from -6 to 6
- win_dout: bfloat16 [16384, 4096], P('seq', 'mp'), may hold values from -16 to 16
- cross_query: bfloat16 [16384, 4096], P('seq', 'mp'), may hold values from -8 to 8
- cross_dout: bfloat16 [16384, 4096], P('seq', 'mp'), may hold values from -16 to 16
- patch_key: bfloat16 [4096, 4096], P('seq', 'mp'), may hold values from -8 to 8
- patch_value: bfloat16 [4096, 4096], P('seq', 'mp'), may hold values from -6 to 6
- patch_len: int32 [64, 64], P('seq'), may hold values from 1 to 16, 256 in all within a row
- patch_owner: int32 [4096, 1], P('seq'), may hold values from 0 to 31; in each aligned block of 128 rows (0 to 127, 128 to 255, ...) at most 8 rows name the same one
- w_query: bfloat16 [4096, 4096], P('seq', 'mp'), may hold values from -0.09375 to 0.09375
Outputs:
- win_dq: bfloat16 [16384, 4096], P('seq', 'mp')
- win_dk: bfloat16 [16384, 4096], P('seq', 'mp')
- win_dv: bfloat16 [16384, 4096], P('seq', 'mp')
- patch_grads: bfloat16 [2, 8192, 4096], P(None, 'seq', 'mp')
- byte_grads: bfloat16 [16384, 4096], P('seq', 'mp')
Inputs may be any that keep to these rules, and one draw needn't show every extreme that they name: `patch_len`: each row lists the byte lengths of the patches of one stored block in order; they sum to 256 and the largest is exactly 16. `patch_owner`: within each aligned block of 128 rows (the patch rows of one device) no owner is named more than 8 times, a bound that some block reaches.
All inputs are finite; a program needn't handle non-finite values.
Results may differ from a plain program's by a relative error of at most 0.017.
Values may be sent and summed in bfloat16 or wider, within the bound.
No kernel may reach another device: no remote copies, remote signals or barrier semaphores. Data moves between devices by JAX's collectives and lax.ppermute only.
A program may use at most 64 MiB of HBM per device.

v0:
```python
import math
import jax
import jax.numpy as jnp
from jax import lax
from jax.sharding import PartitionSpec as P

HD = 128
WIN = 256


def shifted(block, axis, distance):
    devices = range(lax.axis_size(axis))
    route = [(i - distance, i) for i in devices if i - distance in devices]
    return lax.ppermute(block, axis, route)


def head_split(values):
    return values.reshape(values.shape[0], values.shape[1] // HD, HD)


def row_stats(scores, allowed):
    masked = jnp.where(allowed, scores, -1e30)
    row_top = jnp.max(masked, axis=-1, keepdims=True)
    row_total = jnp.sum(
        jnp.exp(jnp.where(allowed, scores - row_top, -1e30)), axis=-1, keepdims=True
    )
    return row_top + jnp.log(row_total)


def window_part(query_rows, dout_rows, key_ext, value_ext, tail_valid):
    window = WIN
    inv_root = 1.0 / math.sqrt(HD)
    length = query_rows.shape[0]
    width = query_rows.shape[1]
    head_count = width // HD
    query_heads = head_split(query_rows)
    dout_heads = head_split(dout_rows)
    key_heads = head_split(key_ext)
    value_heads = head_split(value_ext)
    rows_at = lax.broadcasted_iota(jnp.int32, (window, 2 * window), 0)
    cols_at = lax.broadcasted_iota(jnp.int32, (window, 2 * window), 1)
    gap = cols_at - rows_at

    def one_step(sub_step, state_in):
        dq_acc, dk_acc, dv_acc, total_acc, delta_acc = state_in
        offset = sub_step * window
        allowed = ((gap >= 0) & (gap <= window) & ((cols_at + offset >= window) | tail_valid))[None]
        scores = (
            jnp.einsum("qhd,khd->hqk", query_heads, key_heads, preferred_element_type=jnp.float32)
            * inv_root
        )
        log_total = row_stats(scores, allowed)
        prob_rows = jnp.exp(jnp.where(allowed, scores - log_total, -1e30))
        dprobs = jnp.einsum(
            "qhd,khd->hqk", dout_heads, value_heads, preferred_element_type=jnp.float32
        )
        row_delta = jnp.sum(prob_rows * dprobs, axis=-1, keepdims=True)
        grad_scores = (prob_rows * (dprobs - row_delta) * inv_root).astype(jnp.bfloat16)
        probs_low = prob_rows.astype(jnp.bfloat16)
        dq_sub = jnp.einsum(
            "hqk,khd->qhd", grad_scores, key_heads, preferred_element_type=jnp.float32
        )
        dk_sub = jnp.einsum(
            "hqk,qhd->khd", grad_scores, query_heads, preferred_element_type=jnp.float32
        )
        dv_sub = jnp.einsum(
            "hqk,qhd->khd", probs_low, dout_heads, preferred_element_type=jnp.float32
        )
        dq_acc = dq_sub
        dk_acc = dk_acc + dk_sub
        dv_acc = dv_acc + dv_sub
        total_acc = log_total[:, :, 0].T
        delta_acc = row_delta[:, :, 0].T
        return (dq_acc, dk_acc, dv_acc, total_acc, delta_acc)

    start_state = (
        jnp.zeros((length, head_count, HD), jnp.float32),
        jnp.zeros((length + window, head_count, HD), jnp.float32),
        jnp.zeros((length + window, head_count, HD), jnp.float32),
        jnp.zeros((length, head_count), jnp.float32),
        jnp.zeros((length, head_count), jnp.float32),
    )
    dq_acc, dk_acc, dv_acc, total_acc, delta_acc = lax.fori_loop(
        0, length // window, one_step, start_state
    )
    return (
        dq_acc.reshape(length, width),
        dk_acc.reshape(length + window, width),
        dv_acc.reshape(length + window, width),
        total_acc,
        delta_acc,
    )


def local(
    win_query,
    win_key,
    win_value,
    win_dout,
    cross_query,
    cross_dout,
    patch_key,
    patch_value,
    patch_len,
    patch_owner,
    w_query,
):
    window = WIN
    row_count = win_query.shape[0]
    block_rows = row_count // 2
    width = win_query.shape[1]
    head_count = width // HD
    inv_root = 1.0 / math.sqrt(HD)
    seq_count = lax.axis_size("seq")
    seq_index = lax.axis_index("seq")
    is_last = seq_index == seq_count - 1
    low_valid = seq_index > 0
    low_rim = jnp.stack(
        [win_key[block_rows - window : block_rows], win_value[block_rows - window : block_rows]]
    )
    high_rim = jnp.stack([win_key[row_count - window :], win_value[row_count - window :]])
    from_before = shifted(low_rim, "seq", 1)
    from_after = shifted(high_rim, "seq", -1)
    high_prev = jnp.where(is_last, low_rim, from_after)
    low_part = window_part(
        win_query[:block_rows],
        win_dout[:block_rows],
        jnp.concatenate([from_before[0], win_key[:block_rows]], axis=0),
        jnp.concatenate([from_before[1], win_value[:block_rows]], axis=0),
        low_valid,
    )
    high_part = window_part(
        win_query[block_rows:],
        win_dout[block_rows:],
        jnp.concatenate([high_prev[0], win_key[block_rows:]], axis=0),
        jnp.concatenate([high_prev[1], win_value[block_rows:]], axis=0),
        jnp.array(True),
    )
    low_send = jnp.stack([low_part[1][:window], low_part[2][:window]])
    high_send = jnp.stack([high_part[1][:window], high_part[2][:window]])
    low_back = shifted(low_send.astype(jnp.bfloat16), "seq", -1).astype(low_send.dtype)
    high_back = shifted(high_send.astype(jnp.bfloat16), "seq", 1).astype(high_send.dtype)
    low_extra = low_back + jnp.where(is_last, high_send, 0.0)
    dk_low = low_part[1][window:].at[block_rows - window :].add(low_extra[0])
    dv_low = low_part[2][window:].at[block_rows - window :].add(low_extra[1])
    dk_high = high_part[1][window:].at[block_rows - window :].add(high_back[0])
    dv_high = high_part[2][window:].at[block_rows - window :].add(high_back[1])
    win_dq = jnp.concatenate([low_part[0], high_part[0]], axis=0).astype(jnp.bfloat16)
    win_dk = jnp.concatenate([dk_low, dk_high], axis=0).astype(jnp.bfloat16)
    win_dv = jnp.concatenate([dv_low, dv_high], axis=0).astype(jnp.bfloat16)
    patch_rows = patch_key.shape[0]
    per_block = patch_rows // 2
    cross_heads = cross_query.reshape(2, block_rows, head_count, HD)
    grad_heads = cross_dout.reshape(2, block_rows, head_count, HD)
    key_heads = patch_key.reshape(2, per_block, head_count, HD)
    value_heads = patch_value.reshape(2, per_block, head_count, HD)
    starts = jnp.cumsum(patch_len, axis=1) - patch_len
    within = lax.broadcasted_iota(jnp.int32, (block_rows, per_block), 0)
    allowed = (starts[:, None, :] <= within[None])[:, None]
    scores = (
        jnp.einsum("bqhd,bkhd->bhqk", cross_heads, key_heads, preferred_element_type=jnp.float32)
        * inv_root
    )
    log_total = row_stats(scores, allowed)
    prob_rows = jnp.exp(jnp.where(allowed, scores - log_total, -1e30))
    dprobs = jnp.einsum(
        "bqhd,bkhd->bhqk", grad_heads, value_heads, preferred_element_type=jnp.float32
    )
    row_delta = jnp.sum(prob_rows * dprobs, axis=-1, keepdims=True)
    cross_grad = (prob_rows * (dprobs - row_delta) * inv_root).astype(jnp.bfloat16)
    cross_low = prob_rows.astype(jnp.bfloat16)
    cross_dq = (
        jnp.einsum("bhqk,bkhd->bqhd", cross_grad, key_heads, preferred_element_type=jnp.float32)
        .astype(jnp.bfloat16)
        .reshape(row_count, width)
    )
    patch_dk = (
        jnp.einsum("bhqk,bqhd->bkhd", cross_grad, cross_heads, preferred_element_type=jnp.float32)
        .astype(jnp.bfloat16)
        .reshape(patch_rows, width)
    )
    patch_dv = (
        jnp.einsum("bhqk,bqhd->bkhd", cross_low, grad_heads, preferred_element_type=jnp.float32)
        .astype(jnp.bfloat16)
        .reshape(patch_rows, width)
    )
    stacked = jnp.stack([patch_dk, patch_dv])
    slot_cap = max(2, 2 * (patch_rows // seq_count))
    owners = patch_owner[:, 0]
    onehot = (
        owners[:, None] == lax.broadcasted_iota(jnp.int32, (patch_rows, seq_count), 1)
    ).astype(jnp.int32)
    slot_rank = jnp.sum(onehot * (jnp.cumsum(onehot, axis=0) - onehot), axis=1)
    slot_index = owners * slot_cap + slot_rank
    selector = (
        lax.broadcasted_iota(jnp.int32, (seq_count * slot_cap, patch_rows), 0)
        == slot_index[None, :]
    ).astype(jnp.bfloat16)
    buffer = jnp.einsum(
        "sr,krw->ksw", selector, stacked, preferred_element_type=jnp.float32
    ).astype(jnp.bfloat16)
    buffer = buffer.reshape(2, seq_count, slot_cap, width)
    arrived = lax.all_to_all(buffer, "seq", split_axis=1, concat_axis=1, tiled=True)
    patch_grads = arrived.reshape(2, seq_count * slot_cap, width)
    partial_sums = lax.dot_general(
        cross_dq,
        lax.all_gather(w_query, "seq", axis=0, tiled=True),
        (((1,), (1,)), ((), ())),
        preferred_element_type=jnp.float32,
    )
    byte_grads = lax.psum_scatter(
        partial_sums.astype(jnp.bfloat16), "mp", scatter_dimension=1, tiled=True
    )
    return (win_dq, win_dk, win_dv, patch_grads, byte_grads)


def solution(mesh):
    in_specs = (
        P("seq", "mp"),
        P("seq", "mp"),
        P("seq", "mp"),
        P("seq", "mp"),
        P("seq", "mp"),
        P("seq", "mp"),
        P("seq", "mp"),
        P("seq", "mp"),
        P("seq", None),
        P("seq", None),
        P("seq", "mp"),
    )
    out_specs = (
        P("seq", "mp"),
        P("seq", "mp"),
        P("seq", "mp"),
        P(None, "seq", "mp"),
        P("seq", "mp"),
    )
    return jax.shard_map(local, mesh=mesh, in_specs=in_specs, out_specs=out_specs, check_vma=False)
```

profile of v0, /device:TPU:102, one launch (start us, length us, event | category | flops | bytes accessed | tf_op | source)
XLA Modules:
  0.0 195.4 jit_solution(15188983516557459057)
XLA Ops:
  8.0 1.1 fusion.173
  9.2 1.1 fusion.172
  11.4 2.7 %collective-permute-start.1 = (bf16[2,256,512]{1,2,0:T(8,128)(2,1)}, bf16[2,256,512]{1,2,0:T(8,128)(2,1)S(1)}, u32[]{:S(2)}, u32[]{:S(2)}) collective-permute-start(bf16[2,256,512]{1,2,0:T(8,128)(2,1)} %pad_maximum_fusion.3), channel_id=1, source_target_pairs={{8,0},{16,8},{24,16},{32,24},{40,32},{48,40},{56,48},{64,56},{72,6... | collective-permute-start | bytes 1572872 | tf_op jit(solution)/shard_map/ppermute | solution.py:14
  15.5 1.2 select_reduce_fusion
  16.8 1.1 fusion.106
  17.9 2.5 %fusion.22 = bf16[2,256,4,128]{3,1,2,0:T(8,128)(2,1)} fusion(f32[2,4,256,64]{2,3,1,0:T(8,128)} %fusion.106, f32[2,4,256,64]{2,3,1,0:T(8,128)S(1)} %get-tuple-element.210, f32[2,4,256]{2,1,0:T(4,128)S(1)} %bitcast.241, pred[2,256,64]{1,2,0:T(8,128)(4,1)S(1)} %iota_compare_fusion.1, bf16[2,64,4,128]{3,2,1,0:T(4,128)(2,1)S(1)} %copy-done.12), kind=kOutput, calls=%fused_computation.39 | convolution fusion | flops 34998336 | bytes 1744896 | tf_op jit(solution)/shard_map/bhqk,bkhd->bqhd/dot_general | solution.py:173
  20.4 2.2 %copy.171 = bf16[2,256,4,128]{3,2,1,0:T(4,128)(2,1)} copy(bf16[2,256,4,128]{3,1,2,0:T(8,128)(2,1)} %fusion.22) | data formatting | bytes 1048576 | tf_op jit(solution)/shard_map/convert_element_type | solution.py:174
  22.7 69.5 %all-gather.2.cloned.1.call-done = bf16[4096,512]{1,0:T(8,128)(2,1)} async-done(((bf16[128,512]{1,0:T(8,128)(2,1)}), bf16[4096,512]{1,0:T(8,128)(2,1)}) %all-gather.2.cloned.1.call-update) | async-done | bytes 4194320 | tf_op jit(solution)/shard_map/all_gather | solution.py:207
  92.2 6.7 %convolution_convert_fusion = bf16[512,4096]{1,0:T(8,128)(2,1)} fusion(bf16[4096,512]{1,0:T(8,128)(2,1)} %all-gather.2.cloned.1.call-done, bf16[64,8,4,128]{3,2,1,0:T(4,128)(2,1)} %bitcast.232), kind=kOutput, calls=%fused_computation.3 | convolution fusion | flops 2149580800 | bytes 8912896 | tf_op jit(solution)/shard_map/dot_general | solution.py:205
  99.3 1.6 fusion.27
  101.9 0.9 copy.168
  102.8 8.0 %all-to-all-start = ((bf16[2,32,8,512]{3,2,0,1:T(8,128)(2,1)}), bf16[2,32,8,512]{3,2,0,1:T(8,128)(2,1)S(1)}, u32[]{:S(2)}, u32[]{:S(2)}) async-start(bf16[2,32,8,512]{3,2,0,1:T(8,128)(2,1)} %copy.168), calls=%async_computation | async-start | bytes 1048576 | tf_op jit(solution)/shard_map/all_to_all | solution.py:203
  110.8 1.1 fusion.170
  111.9 1.1 fusion.169
  113.1 0.8 copy.149
  114.2 0.8 copy.192
  116.0 0.9 copy.137
  116.9 0.8 copy.188
  119.4 0.9 pad_maximum_fusion.1
  120.3 0.8 copy.148
  121.2 0.8 copy.144
  122.0 1.7 fusion.6
  124.2 1.8 fusion.98
  125.9 1.7 convolution_bitcast_fusion
  127.7 3.8 %convolution_convert_fusion.3 = bf16[4,256,128]{1,2,0:T(8,128)(2,1)S(1)} fusion(f32[4,512,256]{2,1,0:T(8,128)} %fusion.98, f32[4,512,256]{2,1,0:T(8,128)S(1)} %get-tuple-element.206, f32[4,256]{1,0:T(4,128)S(1)} %log_add_fusion.1, pred[256,512]{0,1:T(8,128)(4,1)S(1)} %copy-done.3, bf16[256,4,128]{2,0,1:T(8,128)(2,1)} %copy.145, bf16[256,4,128]{2,0,1:T(8,128)(2,1)} %copy.144), kind=kOutput, calls=%fused_computation.45 | convolution fusion | flops 141166080 | bytes 5115904 | tf_op jit(solution)/shard_map/while/body/eval_jaxpr/hqk,khd->qhd/dot_general | solution.py:60
  131.5 0.8 copy.155
  132.4 4.7 %collective-permute-start = (bf16[2,256,512]{1,2,0:T(8,128)(2,1)}, bf16[2,256,512]{1,2,0:T(8,128)(2,1)}, u32[]{:S(2)}, u32[]{:S(2)}) collective-permute-start(bf16[2,256,512]{1,2,0:T(8,128)(2,1)} %get-tuple-element.195), channel_id=1, source_target_pairs={{0,8},{8,16},{16,24},{24,32},{32,40},{40,48},{48,56},{56,64},{64,7... | collective-permute-start | bytes 1572872 | tf_op jit(solution)/shard_map/ppermute | solution.py:14
  137.1 2.1 %fusion.166 = (f32[256,4,128]{0,2,1:T(8,128)}, f32[256,4,128]{0,2,1:T(8,128)S(1)}) fusion(f32[512,4,128]{0,2,1:T(8,128)} %convolution_bitcast_fusion), kind=kLoop, calls=%fused_computation.190 | loop fusion | bytes 2097152 | tf_op jit(solution)/shard_map/slice | solution.py:147
  139.2 5.0 %convolution_bitcast_fusion.1 = f32[512,4,128]{0,2,1:T(8,128)} fusion(bf16[256,4,128]{0,2,1:T(8,128)(2,1)} %bitcast.236, f32[4,512,256]{2,1,0:T(8,128)} %fusion.98, f32[4,512,256]{2,1,0:T(8,128)S(1)} %get-tuple-element.206, f32[4,256]{1,0:T(4,128)S(1)} %log_add_fusion.1, pred[256,512]{0,1:T(8,128)(4,1)} %fusion.104), kind=kOutput, calls=%fused_computation.33 | convolution fusion | flops 139986432 | bytes 5640192 | tf_op jit(solution)/shard_map/while/body/eval_jaxpr/hqk,qhd->khd/dot_general | solution.py:63
  144.2 2.1 %fusion.167 = (f32[256,4,128]{0,2,1:T(8,128)}, f32[256,4,128]{0,2,1:T(8,128)S(1)}) fusion(f32[512,4,128]{0,2,1:T(8,128)} %convolution_bitcast_fusion.1), kind=kLoop, calls=%fused_computation.191 | loop fusion | bytes 2097152 | tf_op jit(solution)/shard_map/slice | solution.py:146
  146.3 0.9 fusion.83
  147.2 3.3 %collective-permute-start.3 = (bf16[2,256,512]{1,2,0:T(8,128)(2,1)}, bf16[2,256,512]{1,2,0:T(8,128)(2,1)}, u32[]{:S(2)}, u32[]{:S(2)}) collective-permute-start(bf16[2,256,512]{1,2,0:T(8,128)(2,1)} %fusion.83), channel_id=1, source_target_pairs={{0,8},{8,16},{16,24},{24,32},{32,40},{40,48},{48,56},{56,64},{64,7... | collective-permute-start | bytes 1572872 | tf_op jit(solution)/shard_map/ppermute | solution.py:14
  151.4 1.8 fusion.168
  154.0 1.6 fusion.15
  157.5 0.8 slice.190
  158.3 1.8 copy.136
  160.1 2.8 %fusion.94 = f32[4,512,256]{2,1,0:T(8,128)} fusion(bf16[256,4,128]{0,2,1:T(8,128)(2,1)S(1)} %bitcast.222, bf16[256,4,128]{2,0,1:T(8,128)(2,1)} %copy.137, bf16[256,4,128]{2,0,1:T(8,128)(2,1)} %copy.136), kind=kOutput, calls=%fused_computation.107 | convolution fusion | flops 135266304 | bytes 2883584 | tf_op jit(solution)/shard_map/while/body/eval_jaxpr/qhd,khd->hqk/dot_general | solution.py:54
  163.0 4.7 %convolution_bitcast_fusion.3 = f32[512,4,128]{0,2,1:T(8,128)} fusion(bf16[256,4,128]{0,2,1:T(8,128)(2,1)} %bitcast.234, f32[4,512,256]{2,1,0:T(8,128)} %fusion.94, f32[4,512,256]{2,1,0:T(8,128)S(1)} %get-tuple-element.208, f32[4,256]{1,0:T(4,128)S(1)} %log_add_fusion.2, pred[256,512]{0,1:T(8,128)(4,1)S(1)} %broadcast_and_fusion), kind=kOutput, calls=%fused_computation.35 | convolution fusion | flops 139986432 | bytes 5640192 | tf_op jit(solution)/shard_map/while/body/eval_jaxpr/hqk,qhd->khd/dot_general | solution.py:63
  167.7 1.1 slice.217
  168.8 0.8 pad_maximum_fusion.6
  169.6 2.5 %collective-permute-start.2 = (bf16[2,256,512]{1,2,0:T(8,128)(2,1)}, bf16[2,256,512]{1,2,0:T(8,128)(2,1)}, u32[]{:S(2)}, u32[]{:S(2)}) collective-permute-start(bf16[2,256,512]{1,2,0:T(8,128)(2,1)} %pad_maximum_fusion.6), channel_id=1, source_target_pairs={{8,0},{16,8},{24,16},{32,24},{40,32},{48,40},{56,48},{64,56},{72,6... | collective-permute-start | bytes 1572872 | tf_op jit(solution)/shard_map/ppermute | solution.py:14
  172.1 4.6 %convolution_convert_fusion.4 = bf16[4,128,256]{2,1,0:T(8,128)(2,1)} fusion(f32[4,512,256]{2,1,0:T(8,128)} %fusion.94, f32[4,512,256]{2,1,0:T(8,128)S(1)} %get-tuple-element.208, f32[4,256]{1,0:T(4,128)S(1)} %log_add_fusion.2, pred[256,512]{0,1:T(8,128)(4,1)S(1)} %broadcast_and_fusion, bf16[256,4,128]{2,0,1:T(8,128)(2,1)} %copy.133, ...), kind=kOutput, calls=%fused_computation.46 | convolution fusion | flops 141166080 | bytes 5115904 | tf_op jit(solution)/shard_map/while/body/eval_jaxpr/hqk,khd->qhd/dot_general | solution.py:60
  176.7 1.2 copy.154
  177.9 1.1 convert_element_type.74
  180.1 5.1 %collective-permute-done.2 = bf16[2,256,512]{1,2,0:T(8,128)(2,1)} collective-permute-done((bf16[2,256,512]{1,2,0:T(8,128)(2,1)}, bf16[2,256,512]{1,2,0:T(8,128)(2,1)}, u32[]{:S(2)}, u32[]{:S(2)}) %collective-permute-start.2) | collective-permute-done | bytes 524320 | tf_op jit(solution)/shard_map/ppermute | solution.py:14
  185.1 1.1 select_add_fusion
  186.6 1.0 copy.172
  187.6 1.0 copy.173
  (85 shorter events, 13.1 us)
Async XLA Ops:
  7.2 85.0 %all-gather.2.cloned.1.call-start = ((), (), s32[]{:S(2)}) async-start(), calls=%async_computation.2 | async-start | bytes 4325376 | tf_op jit(solution)/shard_map/all_gather | solution.py:207
  7.9 6.2 %copy-start.8 = (bf16[512,512]{1,0:T(8,128)(2,1)S(1)}, bf16[512,512]{1,0:T(8,128)(2,1)}, u32[]{:S(2)}) copy-start(bf16[512,512]{1,0:T(8,128)(2,1)} %param.32) | copy-start | bytes 1572868
  7.9 180.7 %reduce-scatter.2.cloned.1.call-start = ((), (), s32[]{:S(2)}) async-start(), calls=%async_computation.3 | async-start | bytes 4718592 | tf_op jit(solution)/shard_map/reduce_scatter | solution.py:211
  9.1 5.2 %copy-start.13 = (s32[2,64]{1,0:T(2,128)S(1)}, s32[2,64]{1,0:T(2,128)}, u32[]{:S(2)}) copy-start(s32[2,64]{1,0:T(2,128)} %param.35) | copy-start | bytes 1540
  9.1 5.4 %copy-start.10 = (bf16[128,512]{1,0:T(8,128)(2,1)S(1)}, bf16[128,512]{1,0:T(8,128)(2,1)}, u32[]{:S(2)}) copy-start(bf16[128,512]{1,0:T(8,128)(2,1)} %param.33) | copy-start | bytes 393220
  9.2 6.0 %copy-start.9 = (bf16[512,512]{1,0:T(8,128)(2,1)S(1)}, bf16[512,512]{1,0:T(8,128)(2,1)}, u32[]{:S(2)}) copy-start(bf16[512,512]{1,0:T(8,128)(2,1)} %param.31) | copy-start | bytes 1572868
  10.4 5.0 %copy-start.11 = (bf16[128,512]{1,0:T(8,128)(2,1)S(1)}, bf16[128,512]{1,0:T(8,128)(2,1)}, u32[]{:S(2)}) copy-start(bf16[128,512]{1,0:T(8,128)(2,1)} %param.34) | copy-start | bytes 393220
  11.4 108.0 %collective-permute-start.1 = (bf16[2,256,512]{1,2,0:T(8,128)(2,1)}, bf16[2,256,512]{1,2,0:T(8,128)(2,1)S(1)}, u32[]{:S(2)}, u32[]{:S(2)}) collective-permute-start(bf16[2,256,512]{1,2,0:T(8,128)(2,1)} %pad_maximum_fusion.3), channel_id=1, source_target_pairs={{8,0},{16,8},{24,16},{32,24},{40,32},{48,40},{56,48},{64,56},{72,6... | collective-permute-start | bytes 1572872 | tf_op jit(solution)/shard_map/ppermute | solution.py:14
  15.4 2.6 %copy-start.12 = (bf16[2,64,4,128]{3,2,1,0:T(4,128)(2,1)S(1)}, bf16[2,64,4,128]{3,2,1,0:T(4,128)(2,1)}, u32[]{:S(2)}) copy-start(bf16[2,64,4,128]{3,2,1,0:T(4,128)(2,1)} %reshape.280) | copy-start | bytes 393220
  98.9 2.3 %copy-start.14 = (s32[128,1]{0,1:T(1,128)S(1)}, s32[128,1]{0,1:T(1,128)}, u32[]{:S(2)}) copy-start(s32[128,1]{0,1:T(1,128)} %param.36) | copy-start | bytes 1540
  102.8 47.8 %all-to-all-start = ((bf16[2,32,8,512]{3,2,0,1:T(8,128)(2,1)}), bf16[2,32,8,512]{3,2,0,1:T(8,128)(2,1)S(1)}, u32[]{:S(2)}, u32[]{:S(2)}) async-start(bf16[2,32,8,512]{3,2,0,1:T(8,128)(2,1)} %copy.168), calls=%async_computation | async-start | bytes 1048576 | tf_op jit(solution)/shard_map/all_to_all | solution.py:203
  120.3 1.7 copy-start.3
  122.0 2.1 %copy-start.6 = (bf16[256,4,128]{2,0,1:T(8,128)(2,1)S(1)}, bf16[256,4,128]{2,0,1:T(8,128)(2,1)}, u32[]{:S(2)}) copy-start(bf16[256,4,128]{2,0,1:T(8,128)(2,1)} %copy.149) | copy-start | bytes 786436
  122.0 2.2 %copy-start.7 = (bf16[256,4,128]{2,0,1:T(8,128)(2,1)S(1)}, bf16[256,4,128]{2,0,1:T(8,128)(2,1)}, u32[]{:S(2)}) copy-start(bf16[256,4,128]{2,0,1:T(8,128)(2,1)} %copy.148) | copy-start | bytes 786436
  132.4 19.0 %collective-permute-start = (bf16[2,256,512]{1,2,0:T(8,128)(2,1)}, bf16[2,256,512]{1,2,0:T(8,128)(2,1)}, u32[]{:S(2)}, u32[]{:S(2)}) collective-permute-start(bf16[2,256,512]{1,2,0:T(8,128)(2,1)} %get-tuple-element.195), channel_id=1, source_target_pairs={{0,8},{8,16},{16,24},{24,32},{32,40},{40,48},{48,56},{56,64},{64,7... | collective-permute-start | bytes 1572872 | tf_op jit(solution)/shard_map/ppermute | solution.py:14
  147.2 30.8 %collective-permute-start.3 = (bf16[2,256,512]{1,2,0:T(8,128)(2,1)}, bf16[2,256,512]{1,2,0:T(8,128)(2,1)}, u32[]{:S(2)}, u32[]{:S(2)}) collective-permute-start(bf16[2,256,512]{1,2,0:T(8,128)(2,1)} %fusion.83), channel_id=1, source_target_pairs={{0,8},{8,16},{16,24},{24,32},{32,40},{40,48},{48,56},{56,64},{64,7... | collective-permute-start | bytes 1572872 | tf_op jit(solution)/shard_map/ppermute | solution.py:14
  163.0 5.8 %copy-start.5 = (bf16[256,4,128]{0,2,1:T(8,128)(2,1)S(1)}, bf16[256,4,128]{0,2,1:T(8,128)(2,1)}, u32[]{:S(2)}) copy-start(bf16[256,4,128]{0,2,1:T(8,128)(2,1)} %slice.216) | copy-start | bytes 786436
  169.6 15.5 %collective-permute-start.2 = (bf16[2,256,512]{1,2,0:T(8,128)(2,1)}, bf16[2,256,512]{1,2,0:T(8,128)(2,1)}, u32[]{:S(2)}, u32[]{:S(2)}) collective-permute-start(bf16[2,256,512]{1,2,0:T(8,128)(2,1)} %pad_maximum_fusion.6), channel_id=1, source_target_pairs={{8,0},{16,8},{24,16},{32,24},{40,32},{48,40},{56,48},{64,56},{72,6... | collective-permute-start | bytes 1572872 | tf_op jit(solution)/shard_map/ppermute | solution.py:14
  176.7 2.3 %copy-start.4 = (bf16[256,512]{1,0:T(8,128)(2,1)S(1)}, bf16[256,512]{1,0:T(8,128)(2,1)}, u32[]{:S(2)}) copy-start(bf16[256,512]{1,0:T(8,128)(2,1)} %copy.155) | copy-start | bytes 786436
  176.7 3.2 %copy-start.1 = (f32[256,4,128]{0,2,1:T(8,128)S(1)}, f32[256,4,128]{0,2,1:T(8,128)}, u32[]{:S(2)}) copy-start(f32[256,4,128]{0,2,1:T(8,128)} %get-tuple-element.187) | copy-start | bytes 1572868
  176.7 3.2 %copy-start.2 = (f32[256,4,128]{0,2,1:T(8,128)S(1)}, f32[256,4,128]{0,2,1:T(8,128)}, u32[]{:S(2)}) copy-start(f32[256,4,128]{0,2,1:T(8,128)} %get-tuple-element.189) | copy-start | bytes 1572868
  179.9 6.4 %copy-start = (f32[256,4,128]{0,2,1:T(8,128)S(1)}, f32[256,4,128]{0,2,1:T(8,128)}, u32[]{:S(2)}) copy-start(f32[256,4,128]{0,2,1:T(8,128)} %slice.190) | copy-start | bytes 1572868
  179.9 6.4 %slice-start = ((f32[512,4,128]{0,2,1:T(8,128)}), f32[256,4,128]{0,2,1:T(8,128)S(1)}, s32[]{:S(2)}) async-start(f32[512,4,128]{0,2,1:T(8,128)} %convolution_bitcast_fusion.3), calls=%async_computation.4 | async-start | bytes 1048576 | tf_op jit(solution)/shard_map/slice | solution.py:144
Sparse Core Ops, SparseCore 0:
  10.6 81.5 all-gather.1
  99.0 40.1 reduce-scatter.1
where the time goes:
time: 196 us; the launch traced here: 195 us
  waiting for transfers between devices  75.3 us (38%)
  matrix products  42.1 us (21%)
  local copies, waits for them, and re-layouts  32.6 us (17%)
  starting transfers between devices  21.4 us (11%)
  between operations  14.5 us (7%)
  other arithmetic  9.56 us (5%)
    all_gather x1, waiting for transfers between devices, local(): lax.all_gather(w_query, 'seq', axis=0, tiled=True)  69.5 us
    ppermute x4, starting transfers between devices, shifted(): return lax.ppermute(block, axis, route)  13.3 us
    dot_general x2, matrix products, one_step(): jnp.einsum('hqk,qhd->khd', grad_scores, query_heads, preferred_element_ty...  9.7 us
    dot_general x2, matrix products, one_step(): jnp.einsum('hqk,khd->qhd', grad_scores, key_heads, preferred_element_type...  8.45 us
    all_to_all x1, starting transfers between devices, local(): lax.all_to_all(buffer, 'seq', split_axis=1, concat_axis=1, tiled=True)  8.02 us
    dot_general x1, matrix products, local(): lax.dot_general(cross_dq, lax.all_gather(w_query, 'seq', axis=0, tiled=Tr...  6.66 us
    ppermute x4, waiting for transfers between devices, shifted(): return lax.ppermute(block, axis, route)  5.07 us
    dot_general x2, matrix products, one_step(): jnp.einsum('qhd,khd->hqk', dout_heads, value_heads, preferred_element_typ...  4.6 us
  transfers between devices with their start and end apart: 7, of which 2 were waited for; matrix products, arithmetic and copies ran while one was open for 43% of the time, Pallas kernels for 0%

commit v1 on v0

--- a/solution.py
+++ b/solution.py
@@ -204,7 +204,9 @@
     patch_grads = arrived.reshape(2, seq_count * slot_cap, width)
     partial_sums = lax.dot_general(
         cross_dq,
-        lax.all_gather(w_query, "seq", axis=0, tiled=True),
+        jnp.concatenate(
+            lax.all_to_all(jnp.stack([w_query] * lax.axis_size("seq")), "seq", 0, 0), axis=0
+        ),
         (((1,), (1,)), ((), ())),
         preferred_element_type=jnp.float32,
     )

time: 196 us -> 233 us (1.19)
  waiting for transfers between devices: 75.3 us -> 111 us
  starting transfers between devices: 21.4 us -> 28.5 us
  matrix products: 42.1 us -> 36.7 us
    all_to_all x0 -> x1, waiting for transfers between devices: none -> 90.7 us  [local(): lax.all_to_all(jnp.stack([w_query] * lax.axis_size('seq')), 'seq', 0, 0)]
    all_gather x1 -> x0, waiting for transfers between devices: 69.5 us -> none  [local(): lax.all_gather(w_query, 'seq', axis=0, tiled=True)]
    ppermute x4, waiting for transfers between devices: 5.07 us -> 19.9 us  [shifted(): return lax.ppermute(block, axis, route)]
    all_to_all x0 -> x1, starting transfers between devices: none -> 10.4 us  [local(): lax.all_to_all(jnp.stack([w_query] * lax.axis_size('seq')), 'seq', 0, 0)]
    another operation x0 -> x1, local copies, waits for them, and re-layouts: none -> 3.3 us  [local(): jnp.stack([w_query] * lax.axis_size('seq'))]
    ppermute x4, starting transfers between devices: 13.3 us -> 10.7 us  [shifted(): return lax.ppermute(block, axis, route)]
    unnamed x40 -> x42, local copies, waits for them, and re-layouts: 4.56 us -> 5.19 us
  transfers between devices with their start and end apart: 7 -> 7, of which waited for: 2 -> 3; matrix products, arithmetic and copies ran while one was open for 43% -> 29% of each run, Pallas kernels for 0% -> 0%
where the time goes in v1:
time: 233 us; the launch traced here: 232 us
  waiting for transfers between devices  111 us (48%)
  matrix products  36.7 us (16%)
  local copies, waits for them, and re-layouts  31.9 us (14%)
  starting transfers between devices  28.5 us (12%)
  between operations  14.5 us (6%)
  other arithmetic  9.57 us (4%)
    all_to_all x1, waiting for transfers between devices, local(): lax.all_to_all(jnp.stack([w_query] * lax.axis_size('seq')), 'seq', 0, 0)  90.7 us
    ppermute x4, waiting for transfers between devices, shifted(): return lax.ppermute(block, axis, route)  19.9 us
    ppermute x4, starting transfers between devices, shifted(): return lax.ppermute(block, axis, route)  10.7 us
    all_to_all x1, starting transfers between devices, local(): lax.all_to_all(jnp.stack([w_query] * lax.axis_size('seq')), 'seq', 0, 0)  10.4 us
    dot_general x2, matrix products, one_step(): jnp.einsum('hqk,qhd->khd', grad_scores, query_heads, preferred_element_ty...  9.63 us
    dot_general x2, matrix products, one_step(): jnp.einsum('hqk,khd->qhd', grad_scores, key_heads, preferred_element_type...  8.4 us
    all_to_all x1, starting transfers between devices, local(): lax.all_to_all(buffer, 'seq', split_axis=1, concat_axis=1, tiled=True)  7.41 us
    dot_general x1, matrix products, local(): lax.dot_general(cross_dq, jnp.concatenate(lax.all_to_all(jnp.stack([w_que...  6.5 us
  transfers between devices with their start and end apart: 7, of which 3 were waited for; matrix products, arithmetic and copies ran while one was open for 29% of the time, Pallas kernels for 0%

profile of v1, /device:TPU:102, one launch (start us, length us, event | category | flops | bytes accessed | tf_op | source)
XLA Modules:
  0.0 231.8 jit_solution(6609567802311444625)
XLA Ops:
  7.2 3.3 %stack.44 = bf16[32,128,512]{2,1,0:T(8,128)(2,1)} broadcast(bf16[128,512]{1,0:T(8,128)(2,1)} %param.37), dimensions={1,2} | broadcast | bytes 4325376 | tf_op jit(solution)/shard_map/stack | solution.py:208
  10.5 10.4 %all-to-all-start.1 = ((bf16[32,128,512]{2,1,0:T(8,128)(2,1)}), bf16[32,128,512]{2,1,0:T(8,128)(2,1)}, u32[]{:S(2)}, u32[]{:S(2)}) async-start(bf16[32,128,512]{2,1,0:T(8,128)(2,1)} %stack.44), calls=%async_computation.1 | async-start | bytes 8388608 | tf_op jit(solution)/shard_map/all_to_all | solution.py:208
  24.0 90.7 %all-to-all-done.1 = bf16[32,128,512]{2,1,0:T(8,128)(2,1)} async-done(((bf16[32,128,512]{2,1,0:T(8,128)(2,1)}), bf16[32,128,512]{2,1,0:T(8,128)(2,1)}, u32[]{:S(2)}, u32[]{:S(2)}) %all-to-all-start.1) | async-done | bytes 4194336 | tf_op jit(solution)/shard_map/all_to_all | solution.py:208
  114.7 6.5 %convolution_convert_fusion = bf16[512,4096]{1,0:T(8,128)(2,1)} fusion(bf16[4096,512]{1,0:T(8,128)(2,1)} %bitcast.48, bf16[64,8,4,128]{3,2,1,0:T(4,128)(2,1)S(1)} %bitcast.233), kind=kOutput, calls=%fused_computation.3 | convolution fusion | flops 2149580800 | bytes 8912896 | tf_op jit(solution)/shard_map/dot_general | solution.py:205
  122.9 0.9 copy.168
  123.8 7.4 %all-to-all-start = ((bf16[2,32,8,512]{3,2,0,1:T(8,128)(2,1)}), bf16[2,32,8,512]{3,2,0,1:T(8,128)(2,1)S(1)}, u32[]{:S(2)}, u32[]{:S(2)}) async-start(bf16[2,32,8,512]{3,2,0,1:T(8,128)(2,1)} %copy.168), calls=%async_computation | async-start | bytes 1048576 | tf_op jit(solution)/shard_map/all_to_all | solution.py:203
  131.6 0.8 pad_maximum_fusion.3
  132.5 2.8 %collective-permute-start.1 = (bf16[2,256,512]{1,2,0:T(8,128)(2,1)}, bf16[2,256,512]{1,2,0:T(8,128)(2,1)S(1)}, u32[]{:S(2)}, u32[]{:S(2)}) collective-permute-start(bf16[2,256,512]{1,2,0:T(8,128)(2,1)} %pad_maximum_fusion.3), channel_id=1, source_target_pairs={{8,0},{16,8},{24,16},{32,24},{40,32},{48,40},{56,48},{64,56},{72,6... | collective-permute-start | bytes 1572872 | tf_op jit(solution)/shard_map/ppermute | solution.py:14
  135.2 1.1 fusion.169
  136.3 1.1 fusion.170
  137.4 0.9 copy.188
  138.2 0.8 copy.192
  139.2 0.8 copy.133
  140.1 0.9 copy.145
  141.1 0.8 copy.149
  141.9 0.8 copy.137
  143.9 12.9 %collective-permute-done.1 = bf16[2,256,512]{1,2,0:T(8,128)(2,1)S(1)} collective-permute-done((bf16[2,256,512]{1,2,0:T(8,128)(2,1)}, bf16[2,256,512]{1,2,0:T(8,128)(2,1)S(1)}, u32[]{:S(2)}, u32[]{:S(2)}) %collective-permute-start.1) | collective-permute-done | bytes 524320 | tf_op jit(solution)/shard_map/ppermute | solution.py:14
  156.8 0.9 pad_maximum_fusion.1
  157.7 0.8 copy.144
  158.5 0.8 copy.148
  159.4 2.1 collective-permute-start
  161.5 1.6 fusion.6
  163.6 1.8 fusion.98
  165.4 1.7 convolution_bitcast_fusion
  167.1 3.8 %convolution_convert_fusion.3 = bf16[4,256,128]{1,2,0:T(8,128)(2,1)S(1)} fusion(f32[4,512,256]{2,1,0:T(8,128)} %fusion.98, f32[4,512,256]{2,1,0:T(8,128)S(1)} %get-tuple-element.206, f32[4,256]{1,0:T(4,128)S(1)} %log_add_fusion.1, pred[256,512]{0,1:T(8,128)(4,1)S(1)} %copy-done.3, bf16[256,4,128]{2,0,1:T(8,128)(2,1)} %copy.145, bf16[256,4,128]{2,0,1:T(8,128)(2,1)} %copy.144), kind=kOutput, calls=%fused_computation.45 | convolution fusion | flops 141166080 | bytes 5115904 | tf_op jit(solution)/shard_map/while/body/eval_jaxpr/hqk,khd->qhd/dot_general | solution.py:60
  170.9 0.9 copy.155
  171.7 2.1 fusion.166
  173.8 4.9 %convolution_bitcast_fusion.1 = f32[512,4,128]{0,2,1:T(8,128)} fusion(bf16[256,4,128]{0,2,1:T(8,128)(2,1)} %bitcast.237, f32[4,512,256]{2,1,0:T(8,128)} %fusion.98, f32[4,512,256]{2,1,0:T(8,128)S(1)} %get-tuple-element.206, f32[4,256]{1,0:T(4,128)S(1)} %log_add_fusion.1, pred[256,512]{0,1:T(8,128)(4,1)} %fusion.104), kind=kOutput, calls=%fused_computation.33 | convolution fusion | flops 139986432 | bytes 5640192 | tf_op jit(solution)/shard_map/while/body/eval_jaxpr/hqk,qhd->khd/dot_general | solution.py:63
  178.7 2.1 fusion.167
  180.8 0.9 fusion.83
  181.7 1.9 collective-permute-start.3
  184.4 1.8 fusion.168
  186.2 0.9 copy.132
  187.1 1.6 fusion.15
  190.6 0.8 slice.190
  191.4 1.8 copy.136
  193.2 2.8 %fusion.94 = f32[4,512,256]{2,1,0:T(8,128)} fusion(bf16[256,4,128]{0,2,1:T(8,128)(2,1)S(1)} %bitcast.223, bf16[256,4,128]{2,0,1:T(8,128)(2,1)} %copy.137, bf16[256,4,128]{2,0,1:T(8,128)(2,1)} %copy.136), kind=kOutput, calls=%fused_computation.107 | convolution fusion | flops 135266304 | bytes 2883584 | tf_op jit(solution)/shard_map/while/body/eval_jaxpr/qhd,khd->hqk/dot_general | solution.py:54
  196.0 4.7 %convolution_bitcast_fusion.3 = f32[512,4,128]{0,2,1:T(8,128)} fusion(bf16[256,4,128]{0,2,1:T(8,128)(2,1)} %bitcast.235, f32[4,512,256]{2,1,0:T(8,128)} %fusion.94, f32[4,512,256]{2,1,0:T(8,128)S(1)} %get-tuple-element.208, f32[4,256]{1,0:T(4,128)S(1)} %log_add_fusion.2, pred[256,512]{0,1:T(8,128)(4,1)S(1)} %broadcast_and_fusion), kind=kOutput, calls=%fused_computation.35 | convolution fusion | flops 139986432 | bytes 5640192 | tf_op jit(solution)/shard_map/while/body/eval_jaxpr/hqk,qhd->khd/dot_general | solution.py:63
  200.8 1.1 slice.217
  201.8 0.8 pad_maximum_fusion.6
  202.7 3.9 %collective-permute-start.2 = (bf16[2,256,512]{1,2,0:T(8,128)(2,1)}, bf16[2,256,512]{1,2,0:T(8,128)(2,1)}, u32[]{:S(2)}, u32[]{:S(2)}) collective-permute-start(bf16[2,256,512]{1,2,0:T(8,128)(2,1)} %pad_maximum_fusion.6), channel_id=1, source_target_pairs={{8,0},{16,8},{24,16},{32,24},{40,32},{48,40},{56,48},{64,56},{72,6... | collective-permute-start | bytes 1572872 | tf_op jit(solution)/shard_map/ppermute | solution.py:14
  206.6 4.6 %convolution_convert_fusion.4 = bf16[4,128,256]{2,1,0:T(8,128)(2,1)} fusion(f32[4,512,256]{2,1,0:T(8,128)} %fusion.94, f32[4,512,256]{2,1,0:T(8,128)S(1)} %get-tuple-element.208, f32[4,256]{1,0:T(4,128)S(1)} %log_add_fusion.2, pred[256,512]{0,1:T(8,128)(4,1)S(1)} %broadcast_and_fusion, bf16[256,4,128]{2,0,1:T(8,128)(2,1)} %copy.133, ...), kind=kOutput, calls=%fused_computation.46 | convolution fusion | flops 141166080 | bytes 5115904 | tf_op jit(solution)/shard_map/while/body/eval_jaxpr/hqk,khd->qhd/dot_general | solution.py:60
  211.2 1.2 copy.154
  212.4 1.1 convert_element_type.74
  214.6 7.0 %collective-permute-done.2 = bf16[2,256,512]{1,2,0:T(8,128)(2,1)} collective-permute-done((bf16[2,256,512]{1,2,0:T(8,128)(2,1)}, bf16[2,256,512]{1,2,0:T(8,128)(2,1)}, u32[]{:S(2)}, u32[]{:S(2)}) %collective-permute-start.2) | collective-permute-done | bytes 524320 | tf_op jit(solution)/shard_map/ppermute | solution.py:14
  221.6 1.1 select_add_fusion
  223.0 1.0 copy.172
  224.0 1.0 copy.173
  (87 shorter events, 11.0 us)
Async XLA Ops:
  10.5 10.5 %copy-start.14 = (s32[2,64]{1,0:T(2,128)S(1)}, s32[2,64]{1,0:T(2,128)}, u32[]{:S(2)}) copy-start(s32[2,64]{1,0:T(2,128)} %param.35) | copy-start | bytes 1540
  10.5 10.7 %copy-start.12 = (bf16[128,512]{1,0:T(8,128)(2,1)S(1)}, bf16[128,512]{1,0:T(8,128)(2,1)}, u32[]{:S(2)}) copy-start(bf16[128,512]{1,0:T(8,128)(2,1)} %param.33) | copy-start | bytes 393220
  10.5 10.8 %copy-start.13 = (bf16[128,512]{1,0:T(8,128)(2,1)S(1)}, bf16[128,512]{1,0:T(8,128)(2,1)}, u32[]{:S(2)}) copy-start(bf16[128,512]{1,0:T(8,128)(2,1)} %param.34) | copy-start | bytes 393220
  10.5 10.8 %copy-start.8 = (bf16[512,512]{1,0:T(8,128)(2,1)S(1)}, bf16[512,512]{1,0:T(8,128)(2,1)}, u32[]{:S(2)}) copy-start(bf16[512,512]{1,0:T(8,128)(2,1)} %param.31) | copy-start | bytes 1572868
  10.5 11.0 %copy-start.9 = (bf16[512,512]{1,0:T(8,128)(2,1)S(1)}, bf16[512,512]{1,0:T(8,128)(2,1)}, u32[]{:S(2)}) copy-start(bf16[512,512]{1,0:T(8,128)(2,1)} %param.32) | copy-start | bytes 1572868
  10.5 104.2 %all-to-all-start.1 = ((bf16[32,128,512]{2,1,0:T(8,128)(2,1)}), bf16[32,128,512]{2,1,0:T(8,128)(2,1)}, u32[]{:S(2)}, u32[]{:S(2)}) async-start(bf16[32,128,512]{2,1,0:T(8,128)(2,1)} %stack.44), calls=%async_computation.1 | async-start | bytes 8388608 | tf_op jit(solution)/shard_map/all_to_all | solution.py:208
  20.9 204.1 %reduce-scatter.2.cloned.1.call-start = ((), (), s32[]{:S(2)}) async-start(), calls=%async_computation.3 | async-start | bytes 4718592 | tf_op jit(solution)/shard_map/reduce_scatter | solution.py:213
  121.2 0.7 copy-start.15
  121.8 9.4 %copy-start.10 = (bf16[512,512]{1,0:T(8,128)(2,1)S(1)}, bf16[512,512]{1,0:T(8,128)(2,1)}, u32[]{:S(2)}) copy-start(bf16[512,512]{1,0:T(8,128)(2,1)} %param.28) | copy-start | bytes 1572868
  122.6 8.8 %copy-start.11 = (bf16[512,512]{1,0:T(8,128)(2,1)S(1)}, bf16[512,512]{1,0:T(8,128)(2,1)}, u32[]{:S(2)}) copy-start(bf16[512,512]{1,0:T(8,128)(2,1)} %param.29) | copy-start | bytes 1572868
  123.8 59.8 %all-to-all-start = ((bf16[2,32,8,512]{3,2,0,1:T(8,128)(2,1)}), bf16[2,32,8,512]{3,2,0,1:T(8,128)(2,1)S(1)}, u32[]{:S(2)}, u32[]{:S(2)}) async-start(bf16[2,32,8,512]{3,2,0,1:T(8,128)(2,1)} %copy.168), calls=%async_computation | async-start | bytes 1048576 | tf_op jit(solution)/shard_map/all_to_all | solution.py:203
  132.5 24.3 %collective-permute-start.1 = (bf16[2,256,512]{1,2,0:T(8,128)(2,1)}, bf16[2,256,512]{1,2,0:T(8,128)(2,1)S(1)}, u32[]{:S(2)}, u32[]{:S(2)}) collective-permute-start(bf16[2,256,512]{1,2,0:T(8,128)(2,1)} %pad_maximum_fusion.3), channel_id=1, source_target_pairs={{8,0},{16,8},{24,16},{32,24},{40,32},{48,40},{56,48},{64,56},{72,6... | collective-permute-start | bytes 1572872 | tf_op jit(solution)/shard_map/ppermute | solution.py:14
  157.6 3.8 %copy-start.3 = (pred[256,512]{0,1:T(8,128)(4,1)S(1)}, pred[256,512]{0,1:T(8,128)(4,1)}, u32[]{:S(2)}) copy-start(pred[256,512]{0,1:T(8,128)(4,1)} %fusion.104) | copy-start | bytes 393220
  159.4 25.1 %collective-permute-start = (bf16[2,256,512]{1,2,0:T(8,128)(2,1)}, bf16[2,256,512]{1,2,0:T(8,128)(2,1)}, u32[]{:S(2)}, u32[]{:S(2)}) collective-permute-start(bf16[2,256,512]{1,2,0:T(8,128)(2,1)} %get-tuple-element.195), channel_id=1, source_target_pairs={{0,8},{8,16},{16,24},{24,32},{32,40},{40,48},{48,56},{56,64},{64,7... | collective-permute-start | bytes 1572872 | tf_op jit(solution)/shard_map/ppermute | solution.py:14
  161.5 2.1 copy-start.6
  161.5 2.1 copy-start.7
  181.7 30.8 %collective-permute-start.3 = (bf16[2,256,512]{1,2,0:T(8,128)(2,1)}, bf16[2,256,512]{1,2,0:T(8,128)(2,1)}, u32[]{:S(2)}, u32[]{:S(2)}) collective-permute-start(bf16[2,256,512]{1,2,0:T(8,128)(2,1)} %fusion.83), channel_id=1, source_target_pairs={{0,8},{8,16},{16,24},{24,32},{32,40},{40,48},{48,56},{56,64},{64,7... | collective-permute-start | bytes 1572872 | tf_op jit(solution)/shard_map/ppermute | solution.py:14
  196.0 5.8 %copy-start.5 = (bf16[256,4,128]{0,2,1:T(8,128)(2,1)S(1)}, bf16[256,4,128]{0,2,1:T(8,128)(2,1)}, u32[]{:S(2)}) copy-start(bf16[256,4,128]{0,2,1:T(8,128)(2,1)} %slice.216) | copy-start | bytes 786436
  202.7 18.9 %collective-permute-start.2 = (bf16[2,256,512]{1,2,0:T(8,128)(2,1)}, bf16[2,256,512]{1,2,0:T(8,128)(2,1)}, u32[]{:S(2)}, u32[]{:S(2)}) collective-permute-start(bf16[2,256,512]{1,2,0:T(8,128)(2,1)} %pad_maximum_fusion.6), channel_id=1, source_target_pairs={{8,0},{16,8},{24,16},{32,24},{40,32},{48,40},{56,48},{64,56},{72,6... | collective-permute-start | bytes 1572872 | tf_op jit(solution)/shard_map/ppermute | solution.py:14
  211.2 2.3 %copy-start.4 = (bf16[256,512]{1,0:T(8,128)(2,1)S(1)}, bf16[256,512]{1,0:T(8,128)(2,1)}, u32[]{:S(2)}) copy-start(bf16[256,512]{1,0:T(8,128)(2,1)} %copy.155) | copy-start | bytes 786436
  211.2 3.2 %copy-start.1 = (f32[256,4,128]{0,2,1:T(8,128)S(1)}, f32[256,4,128]{0,2,1:T(8,128)}, u32[]{:S(2)}) copy-start(f32[256,4,128]{0,2,1:T(8,128)} %get-tuple-element.187) | copy-start | bytes 1572868
  211.2 3.2 %copy-start.2 = (f32[256,4,128]{0,2,1:T(8,128)S(1)}, f32[256,4,128]{0,2,1:T(8,128)}, u32[]{:S(2)}) copy-start(f32[256,4,128]{0,2,1:T(8,128)} %get-tuple-element.189) | copy-start | bytes 1572868
  214.4 8.3 %copy-start = (f32[256,4,128]{0,2,1:T(8,128)S(1)}, f32[256,4,128]{0,2,1:T(8,128)}, u32[]{:S(2)}) copy-start(f32[256,4,128]{0,2,1:T(8,128)} %slice.190) | copy-start | bytes 1572868
  214.4 8.3 %slice-start = ((f32[512,4,128]{0,2,1:T(8,128)}), f32[256,4,128]{0,2,1:T(8,128)S(1)}, s32[]{:S(2)}) async-start(f32[512,4,128]{0,2,1:T(8,128)} %convolution_bitcast_fusion.3), calls=%async_computation.4 | async-start | bytes 1048576 | tf_op jit(solution)/shard_map/slice | solution.py:144
Sparse Core Ops, SparseCore 0:
  121.3 40.2 reduce-scatter.1
